TPU v7x, 256 devices: a whole 4x4x8 slice. The times are simulated.
256 devices in a mesh: grp: 4 (over z_lo), row: 4 (over x), col: 16 (over y, z_hi, core).
Axes of the slice: x: 4, y: 4, z: 8 (z_hi: 2, z_lo: 4; z = z_hi * 4 + z_lo), core: 2. Of those that a mesh axis runs over, the one named last changes fastest.
Arguments:
- outer_params: float32 [8192, 1024], P('col', 'row'), may hold values from -0.0625 to 0.0625
- first_moment: float32 [4, 8192, 1024], P('grp', 'col', 'row'), may hold values from -0.12 to 0.12
- second_moment: float32 [4, 8192, 1024], P('grp', 'col', 'row'), may hold values from 0.0001 to 0.01
- outer_moment: float32 [8192, 1024], P('col', 'row'), may hold values from -0.06 to 0.06
- activations: bfloat16 [4, 3, 2048, 8192], P('grp', None, 'row', 'col'), may hold values from -6 to 6
- targets: bfloat16 [4, 3, 2048, 1024], P('grp', None, 'col', 'row'), may hold values from -6 to 6
Outputs:
- new_params: float32 [8192, 1024], P('col', 'row')
- new_moment: float32 [8192, 1024], P('col', 'row')
All inputs are finite; a program needn't handle non-finite values.
Results may differ from a plain program's by a relative error of at most 0.0054.
Values may be sent and summed in bfloat16 or wider, within the bound.
A program may use at most 64 MiB of HBM per device.

v0:
```python
import jax
import jax.numpy as jnp
from jax import lax
from jax.sharding import Mesh
from jax.sharding import PartitionSpec as P

TOKENS = 2048
STEPS = 3
SLOW_STEPS = 1
PRIOR = 100
COL = ("col_0", "col_1", "col_2")
beta_first = 0.9
beta_second = 0.95
inner_rate = 0.01
decay_rate = 0.1
epsilon_value = 1e-08
outer_rate = 0.7
momentum_coef = 0.9


def split_up(shard, dim, count):
    before, after = (shard.shape[:dim], shard.shape[dim + 1 :])
    return jnp.moveaxis(shard.reshape(*before, count, -1, *after), dim, 0)


def summed_on_arrival(shard, axis, dim):
    count = lax.axis_size(axis)
    parts = lax.all_to_all(split_up(shard, dim, count), axis, 0, 0, tiled=True)
    return jnp.sum(parts, axis=0)


def sum_in_two_steps(shard, axes, dim):
    far, near = axes
    own = summed_on_arrival(split_up(shard, dim, lax.axis_size(far)), near, dim + 1)
    return jnp.sum(lax.all_to_all(own, far, 0, 0, tiled=True), axis=0)


def filled_up(lines, count):
    spare = -lines.shape[0] % count
    if not spare:
        return lines
    return jnp.concatenate([lines, jnp.zeros((spare, *lines.shape[1:]), lines.dtype)])


def sent_to_all(shard, axis):
    copies = jnp.broadcast_to(shard, (lax.axis_size(axis), *shard.shape))
    return lax.all_to_all(copies, axis, split_axis=0, concat_axis=0, tiled=True)


def in_order(parts, dim):
    shape = list(parts.shape[1:])
    shape[dim] *= parts.shape[0]
    return jnp.moveaxis(parts, 0, dim).reshape(shape)


def whole_of(shard, axes, dim):
    far, near = axes
    parts = sent_to_all(sent_to_all(shard, far), near)
    return in_order(parts.swapaxes(0, 1).reshape(-1, *shard.shape), dim)


def total_of(shard, axes):
    lines = shard.reshape(-1, shard.shape[-1])
    own = sum_in_two_steps(
        filled_up(lines, lax.axis_size(axes[0]) * lax.axis_size(axes[1])), axes, 0
    )
    whole = whole_of(own, axes, 0)
    return whole[: len(lines)].reshape(shard.shape)


def over_copies(shard, axis):
    everything = sent_to_all(shard, axis)
    return jnp.sum(everything, axis=0)


def local(outer_params, first_moment, second_moment, outer_moment, activations, targets):
    unit = lax.axis_index("grp")
    gathered = lax.all_gather(activations[0], "row", axis=1, tiled=True)
    wanted_all = targets[0]
    wanted_all = lax.all_gather(wanted_all, COL, axis=1, tiled=True)
    first = first_moment[0]
    second = second_moment[0]
    params = outer_params
    for inner_step in range(STEPS):
        inputs = gathered[inner_step]
        partial_value = jnp.dot(
            inputs, params.astype(jnp.bfloat16), preferred_element_type=jnp.float32
        )
        output = total_of(partial_value, (("col_0", "col_1"), "col_2"))
        residual = (output - wanted_all[inner_step].astype(jnp.float32)).astype(jnp.bfloat16)
        gradient = (
            lax.dot_general(
                inputs, residual, (((0,), (0,)), ((), ())), preferred_element_type=jnp.float32
            )
            / TOKENS
        )
        first_next = beta_first * first + (1.0 - beta_first) * gradient
        second_next = beta_second * second + (1.0 - beta_second) * gradient * gradient
        power = PRIOR + inner_step + 1
        corrected = (
            first_next
            / (1.0 - beta_first**power)
            / (jnp.sqrt(second_next / (1.0 - beta_second**power)) + epsilon_value)
        )
        params_next = params - inner_rate * (corrected + decay_rate * params)
        active = jnp.logical_or(unit < 3, inner_step < SLOW_STEPS)
        params = jnp.where(active, params_next, params)
        first = jnp.where(active, first_next, first)
        second = jnp.where(active, second_next, second)
    total_steps = float(3 * STEPS + SLOW_STEPS)
    weight = jnp.where(unit < 3, float(STEPS), float(SLOW_STEPS)) / total_steps
    term = weight * (outer_params - params)
    pseudo = over_copies(term, "grp")
    new_moment = momentum_coef * outer_moment + pseudo
    new_params = outer_params - outer_rate * (pseudo + momentum_coef * new_moment)
    return (new_params, new_moment)


def solution(mesh):
    finer = Mesh(
        mesh.devices.reshape(mesh.shape["grp"], mesh.shape["row"], 4, 2, 2),
        ("grp", "row", "col_0", "col_1", "col_2"),
    )
    placed = (
        P(COL, "row"),
        P("grp", COL, "row"),
        P("grp", COL, "row"),
        P(COL, "row"),
        P("grp", None, "row", COL),
        P("grp", None, COL, "row"),
    )
    return jax.shard_map(
        local,
        mesh=finer,
        in_specs=placed,
        out_specs=(P(COL, "row"), P(COL, "row")),
        check_vma=False,
    )
```

profile of v0, /device:TPU:1, one launch (start us, length us, event | category | flops | bytes accessed | tf_op | source)
XLA Modules:
  0.0 409.2 jit_solution(15068283860982565642)
XLA Ops:
  8.7 73.2 %all-gather.5.cloned.1.call-done = bf16[1,3,2048,512]{3,2,1,0:T(8,128)(2,1)} async-done(((bf16[1,3,512,512]{3,2,1,0:T(8,128)(2,1)}), bf16[1,3,2048,512]{3,2,1,0:T(8,128)(2,1)}) %all-gather.5.cloned.1.call-update) | async-done | bytes 6291472 | tf_op jit(solution)/shard_map/all_gather | solution.py:78
  81.8 1.6 slice-done.6
  84.3 5.8 %all_to_all.65 = f32[2,8,128,256]{3,2,1,0:T(8,128)S(1)} all-to-all(f32[2,8,128,256]{3,2,1,0:T(8,128)S(1)} %copy.76), channel_id=1, replica_groups=mesh['grp'=4,'row'=4,'col_0'=4,'col_1'=2,'col_2'=2] {'col_2'}, dimensions={0} | all-to-all | bytes 4194304 | tf_op jit(solution)/shard_map/all_to_all | solution.py:28
  90.3 35.3 %all_to_all.66 = f32[8,128,256]{2,1,0:T(8,128)S(1)} all-to-all(f32[8,128,256]{2,1,0:T(8,128)S(1)} %reduce_sum.63), channel_id=1, replica_groups=mesh['grp'=4,'row'=4,'col_0'=4,'col_1'=2,'col_2'=2] {'col_0','col_1'}, dimensions={0} | all-to-all | bytes 2097152 | tf_op jit(solution)/shard_map/all_to_all | solution.py:35
  125.7 1.1 broadcast_in_dim.21
  126.8 7.7 %all-to-all-start.2 = ((f32[8,128,256]{2,1,0:T(8,128)}), f32[8,128,256]{2,1,0:T(8,128)S(1)}, u32[]{:S(2)}, u32[]{:S(2)}) async-start(f32[8,128,256]{2,1,0:T(8,128)} %broadcast_in_dim.21), calls=%async_computation.2 | async-start | bytes 2097152 | tf_op jit(solution)/shard_map/all_to_all | solution.py:47
  134.8 1.0 copy.75
  136.0 35.4 %all-gather.7.cloned.1.call-done = bf16[1,3,2048,256]{3,2,1,0:T(8,128)(2,1)} async-done(((bf16[1,3,128,256]{3,2,1,0:T(8,128)(2,1)}), bf16[1,3,2048,256]{3,2,1,0:T(8,128)(2,1)}) %all-gather.7.cloned.1.call-update) | async-done | bytes 3145744 | tf_op jit(solution)/shard_map/all_gather | solution.py:80
  171.4 3.4 fusion.43
  175.0 5.7 %all_to_all.67 = f32[2,8,128,256]{3,2,1,0:T(8,128)S(1)} all-to-all(f32[2,8,128,256]{3,2,1,0:T(8,128)S(1)} %broadcast_in_dim.22), channel_id=1, replica_groups=mesh['grp'=4,'row'=4,'col_0'=4,'col_1'=2,'col_2'=2] {'col_2'}, dimensions={0} | all-to-all | bytes 4194304 | tf_op jit(solution)/shard_map/all_to_all | solution.py:47
  182.7 2.4 convolution_bitcast_fusion.1
  185.2 3.0 reshape_reshape.4
  188.3 5.4 %all_to_all.68 = f32[2,8,128,256]{2,1,3,0:T(8,128)S(1)} all-to-all(f32[2,8,128,256]{2,1,3,0:T(8,128)S(1)} %bitcast.148), channel_id=1, replica_groups=mesh['grp'=4,'row'=4,'col_0'=4,'col_1'=2,'col_2'=2] {'col_2'}, dimensions={0} | all-to-all | bytes 4194304 | tf_op jit(solution)/shard_map/all_to_all | solution.py:28
  194.2 21.3 %all_to_all.69 = f32[8,128,256]{1,2,0:T(8,128)S(1)} all-to-all(f32[8,128,256]{1,2,0:T(8,128)S(1)} %copy.83), channel_id=1, replica_groups=mesh['grp'=4,'row'=4,'col_0'=4,'col_1'=2,'col_2'=2] {'col_0','col_1'}, dimensions={0} | all-to-all | bytes 2097152 | tf_op jit(solution)/shard_map/all_to_all | solution.py:35
  215.7 1.0 broadcast_in_dim.23
  216.7 3.6 all-to-all-start.6
  220.3 24.7 %all-to-all-done.6 = f32[8,128,256]{2,1,0:T(8,128)S(1)} async-done(((f32[8,128,256]{2,1,0:T(8,128)}), f32[8,128,256]{2,1,0:T(8,128)S(1)}, u32[]{:S(2)}, u32[]{:S(2)}) %all-to-all-start.6) | async-done | bytes 1048608 | tf_op jit(solution)/shard_map/all_to_all | solution.py:47
  245.2 6.0 %all_to_all.70 = f32[2,8,128,256]{3,2,1,0:T(8,128)S(1)} all-to-all(f32[2,8,128,256]{3,2,1,0:T(8,128)S(1)} %broadcast_in_dim.24), channel_id=1, replica_groups=mesh['grp'=4,'row'=4,'col_0'=4,'col_1'=2,'col_2'=2] {'col_2'}, dimensions={0} | all-to-all | bytes 4194304 | tf_op jit(solution)/shard_map/all_to_all | solution.py:47
  253.1 2.9 convolution_bitcast_fusion
  256.0 3.0 reshape_reshape.5
  259.2 5.4 %all_to_all.71 = f32[2,8,128,256]{2,1,3,0:T(8,128)S(1)} all-to-all(f32[2,8,128,256]{2,1,3,0:T(8,128)S(1)} %bitcast.149), channel_id=1, replica_groups=mesh['grp'=4,'row'=4,'col_0'=4,'col_1'=2,'col_2'=2] {'col_2'}, dimensions={0} | all-to-all | bytes 4194304 | tf_op jit(solution)/shard_map/all_to_all | solution.py:28
  265.1 25.3 %all_to_all.72 = f32[8,128,256]{1,2,0:T(8,128)S(1)} all-to-all(f32[8,128,256]{1,2,0:T(8,128)S(1)} %copy.89), channel_id=1, replica_groups=mesh['grp'=4,'row'=4,'col_0'=4,'col_1'=2,'col_2'=2] {'col_0','col_1'}, dimensions={0} | all-to-all | bytes 2097152 | tf_op jit(solution)/shard_map/all_to_all | solution.py:35
  290.5 1.0 broadcast_in_dim.25
  291.5 3.6 all-to-all-start.10
  295.1 20.5 %all-to-all-done.10 = f32[8,128,256]{2,1,0:T(8,128)S(1)} async-done(((f32[8,128,256]{2,1,0:T(8,128)}), f32[8,128,256]{2,1,0:T(8,128)S(1)}, u32[]{:S(2)}, u32[]{:S(2)}) %all-to-all-start.10) | async-done | bytes 1048608 | tf_op jit(solution)/shard_map/all_to_all | solution.py:47
  315.8 6.9 %all_to_all.73 = f32[2,8,128,256]{3,2,1,0:T(8,128)S(1)} all-to-all(f32[2,8,128,256]{3,2,1,0:T(8,128)S(1)} %broadcast_in_dim.26), channel_id=1, replica_groups=mesh['grp'=4,'row'=4,'col_0'=4,'col_1'=2,'col_2'=2] {'col_2'}, dimensions={0} | all-to-all | bytes 4194304 | tf_op jit(solution)/shard_map/all_to_all | solution.py:47
  324.4 3.4 fusion.8
  328.0 1.5 broadcast_in_dim.27
  329.5 20.7 %all-to-all-start.12 = ((f32[4,512,256]{2,1,0:T(8,128)}), f32[4,512,256]{2,1,0:T(8,128)S(1)}, u32[]{:S(2)}, u32[]{:S(2)}) async-start(f32[4,512,256]{2,1,0:T(8,128)} %broadcast_in_dim.27), calls=%async_computation.12 | async-start | bytes 4194304 | tf_op jit(solution)/shard_map/all_to_all | solution.py:47
  350.3 1.2 copy.95
  351.5 46.5 %all-to-all-done.12 = f32[4,512,256]{2,1,0:T(8,128)S(1)} async-done(((f32[4,512,256]{2,1,0:T(8,128)}), f32[4,512,256]{2,1,0:T(8,128)S(1)}, u32[]{:S(2)}, u32[]{:S(2)}) %all-to-all-start.12) | async-done | bytes 2097184 | tf_op jit(solution)/shard_map/all_to_all | solution.py:47
  399.0 1.2 copy.97
  (90 shorter events, 13.9 us)
Async XLA Ops:
  7.2 74.7 %all-gather.5.cloned.1.call-start = ((), (), s32[]{:S(2)}) async-start(), calls=%async_computation.13 | async-start | bytes 7864320 | tf_op jit(solution)/shard_map/all_gather | solution.py:78
  7.9 163.5 %all-gather.7.cloned.1.call-start = ((), (), s32[]{:S(2)}) async-start(), calls=%async_computation.14 | async-start | bytes 3342336 | tf_op jit(solution)/shard_map/all_gather | solution.py:80
  8.6 73.2 %copy-start.2 = (f32[512,256]{1,0:T(8,128)S(1)}, f32[512,256]{1,0:T(8,128)}, u32[]{:S(2)}) copy-start(f32[512,256]{1,0:T(8,128)} %param.6) | copy-start | bytes 1572868
  81.8 1.6 slice-start.6
  125.6 8.9 %copy-start.3 = (f32[512,256]{1,0:T(8,128)S(1)}, f32[512,256]{1,0:T(8,128)}, u32[]{:S(2)}) copy-start(f32[512,256]{1,0:T(8,128)} %param.6) | copy-start | bytes 1572868
  125.7 9.1 %copy-start.7 = (f32[1,512,256]{2,1,0:T(8,128)S(1)}, f32[1,512,256]{2,1,0:T(8,128)}, u32[]{:S(2)}) copy-start(f32[1,512,256]{2,1,0:T(8,128)} %param.7) | copy-start | bytes 1572868
  126.8 9.0 %copy-start.8 = (f32[1,512,256]{2,1,0:T(8,128)S(1)}, f32[1,512,256]{2,1,0:T(8,128)}, u32[]{:S(2)}) copy-start(f32[1,512,256]{2,1,0:T(8,128)} %param.8) | copy-start | bytes 1572868
  126.8 47.9 %all-to-all-start.2 = ((f32[8,128,256]{2,1,0:T(8,128)}), f32[8,128,256]{2,1,0:T(8,128)S(1)}, u32[]{:S(2)}, u32[]{:S(2)}) async-start(f32[8,128,256]{2,1,0:T(8,128)} %broadcast_in_dim.21), calls=%async_computation.2 | async-start | bytes 2097152 | tf_op jit(solution)/shard_map/all_to_all | solution.py:47
  134.8 47.1 %copy-start.4 = (f32[512,256]{0,1:T(8,128)}, f32[512,256]{0,1:T(8,128)S(1)}, u32[]{:S(2)}) copy-start(f32[512,256]{0,1:T(8,128)S(1)} %copy.98) | copy-start | bytes 1572868
  136.0 45.9 %copy-start.12 = (f32[1,512,256]{1,2,0:T(8,128)}, f32[1,512,256]{1,2,0:T(8,128)S(1)}, u32[]{:S(2)}) copy-start(f32[1,512,256]{1,2,0:T(8,128)S(1)} %copy.78) | copy-start | bytes 1572868
  174.8 6.3 %slice-start = ((s8[6291456]{0:T(1024)(128)(4,1)}), s8[4194304]{0:T(1024)(128)(4,1)S(1)}, s32[]{:S(2)}) async-start(s8[6291456]{0:T(1024)(128)(4,1)} %bitcast.150), calls=%async_computation.15 | async-start | bytes 8388608
  175.0 6.1 %slice-start.1 = ((s8[6291456]{0:T(1024)(128)(4,1)}), s8[2097152]{0:T(1024)(128)(4,1)S(1)}, s32[]{:S(2)}) async-start(s8[6291456]{0:T(1024)(128)(4,1)} %bitcast.150), calls=%async_computation.16 | async-start | bytes 4194304
  181.1 1.6 copy-start.9
  181.9 0.9 copy-start.15
  216.7 28.3 %all-to-all-start.6 = ((f32[8,128,256]{2,1,0:T(8,128)}), f32[8,128,256]{2,1,0:T(8,128)S(1)}, u32[]{:S(2)}, u32[]{:S(2)}) async-start(f32[8,128,256]{2,1,0:T(8,128)} %broadcast_in_dim.23), calls=%async_computation.6 | async-start | bytes 2097152 | tf_op jit(solution)/shard_map/all_to_all | solution.py:47
  245.0 6.5 %slice-start.2 = ((s8[6291456]{0:T(1024)(128)(4,1)}), s8[4194304]{0:T(1024)(128)(4,1)S(1)}, s32[]{:S(2)}) async-start(s8[6291456]{0:T(1024)(128)(4,1)} %bitcast.152), calls=%async_computation.17 | async-start | bytes 8388608
  245.2 6.0 %copy-start.1 = (bf16[1,1,2048,256]{3,2,1,0:T(8,128)(2,1)S(1)}, bf16[1,1,2048,256]{3,2,1,0:T(8,128)(2,1)}, u32[]{:S(2)}) copy-start(bf16[1,1,2048,256]{3,2,1,0:T(8,128)(2,1)} %get-tuple-element.13) | copy-start | bytes 3145732
  245.2 6.3 %slice-start.3 = ((s8[6291456]{0:T(1024)(128)(4,1)}), s8[2097152]{0:T(1024)(128)(4,1)S(1)}, s32[]{:S(2)}) async-start(s8[6291456]{0:T(1024)(128)(4,1)} %bitcast.152), calls=%async_computation.18 | async-start | bytes 4194304
  251.6 1.6 copy-start.5
  251.6 1.6 copy-start.10
  251.6 1.5 copy-start.13
  251.6 1.5 copy-start.16
  291.5 24.0 %all-to-all-start.10 = ((f32[8,128,256]{2,1,0:T(8,128)}), f32[8,128,256]{2,1,0:T(8,128)S(1)}, u32[]{:S(2)}, u32[]{:S(2)}) async-start(f32[8,128,256]{2,1,0:T(8,128)} %broadcast_in_dim.25), calls=%async_computation.10 | async-start | bytes 2097152 | tf_op jit(solution)/shard_map/all_to_all | solution.py:47
  315.6 7.5 %slice-start.4 = ((s8[6291456]{0:T(1024)(128)(4,1)}), s8[4194304]{0:T(1024)(128)(4,1)S(1)}, s32[]{:S(2)}) async-start(s8[6291456]{0:T(1024)(128)(4,1)} %bitcast.154), calls=%async_computation.19 | async-start | bytes 8388608
  315.8 6.9 %copy-start = (bf16[1,1,2048,256]{3,2,1,0:T(8,128)(2,1)S(1)}, bf16[1,1,2048,256]{3,2,1,0:T(8,128)(2,1)}, u32[]{:S(2)}) copy-start(bf16[1,1,2048,256]{3,2,1,0:T(8,128)(2,1)} %get-tuple-element.14) | copy-start | bytes 3145732
  315.8 7.3 %slice-start.5 = ((s8[6291456]{0:T(1024)(128)(4,1)}), s8[2097152]{0:T(1024)(128)(4,1)S(1)}, s32[]{:S(2)}) async-start(s8[6291456]{0:T(1024)(128)(4,1)} %bitcast.154), calls=%async_computation.20 | async-start | bytes 4194304
  322.7 1.0 copy-start.6
  322.7 1.2 copy-start.11
  322.7 1.4 copy-start.14
  322.7 1.5 copy-start.17
  322.8 1.7 copy-start.19
  329.5 68.5 %all-to-all-start.12 = ((f32[4,512,256]{2,1,0:T(8,128)}), f32[4,512,256]{2,1,0:T(8,128)S(1)}, u32[]{:S(2)}, u32[]{:S(2)}) async-start(f32[4,512,256]{2,1,0:T(8,128)} %broadcast_in_dim.27), calls=%async_computation.12 | async-start | bytes 4194304 | tf_op jit(solution)/shard_map/all_to_all | solution.py:47
  (1 other events, 0.8 us)
Sparse Core Ops, SparseCore 0:
  9.8 71.9 all-gather.4
  84.6 86.7 all-gather.6
where the time goes:
time: 410 us; the launch traced here: 409 us
  waiting for transfers between devices  202 us (49%)
  blocking collectives  117 us (29%)
  starting transfers between devices  35.7 us (9%)
  local copies, waits for them, and re-layouts  26.5 us (6%)
  between operations  14.6 us (4%)
  matrix products  10.9 us (3%)
    all_to_all x4, waiting for transfers between devices, sent_to_all(): return lax.all_to_all(copies, axis, split_axis=0, concat_axis=0, tiled=True)  91.7 us
    all_to_all x3, blocking collectives, sum_in_two_steps(): return jnp.sum(lax.all_to_all(own, far, 0, 0, tiled=True), axis=0)  81.9 us
    all_gather x1, waiting for transfers between devices, local(): gathered = lax.all_gather(activations[0], 'row', axis=1, tiled=True)  73.2 us
    all_to_all x4, starting transfers between devices, sent_to_all(): return lax.all_to_all(copies, axis, split_axis=0, concat_axis=0, tiled=True)  35.6 us
    all_gather x1, waiting for transfers between devices, local(): wanted_all = lax.all_gather(wanted_all, COL, axis=1, tiled=True)  35.4 us
    all_to_all x3, blocking collectives, sent_to_all(): return lax.all_to_all(copies, axis, split_axis=0, concat_axis=0, tiled=True)  18.6 us
    all_to_all x3, blocking collectives, summed_on_arrival(): parts = lax.all_to_all(split_up(shard, dim, count), axis, 0, 0, tiled=True)  16.6 us
  transfers between devices with their start and end apart: 6, of which 5 were waited for; matrix products, arithmetic and copies ran while one was open for 2% of the time, Pallas kernels for 0%

commit v1 on v0

--- a/solution.py
+++ b/solution.py
@@ -75,7 +75,25 @@
 
 def local(outer_params, first_moment, second_moment, outer_moment, activations, targets):
     unit = lax.axis_index("grp")
-    gathered = lax.all_gather(activations[0], "row", axis=1, tiled=True)
+    length, mine, rows = (lax.axis_size("row"), lax.axis_index("row"), activations[0].shape[1])
+    right = [(i, (i + 1) % length) for i in range(length)]
+    downward = [(i, (i - 1) % length) for i in range(length)]
+    out = jnp.zeros(
+        (*activations[0].shape[:1], length * rows, *activations[0].shape[1 + 1 :]),
+        activations[0].dtype,
+    )
+    out = lax.dynamic_update_slice_in_dim(out, activations[0], mine * rows, axis=1)
+    from_left = from_right = activations[0]
+    half = length // 2
+    for hop in range(1, half + 1):
+        from_left = lax.ppermute(from_left, "row", right)
+        out = lax.dynamic_update_slice_in_dim(out, from_left, (mine - hop) % length * rows, axis=1)
+        if hop < length - half:
+            from_right = lax.ppermute(from_right, "row", downward)
+            out = lax.dynamic_update_slice_in_dim(
+                out, from_right, (mine + hop) % length * rows, axis=1
+            )
+    gathered = out
     wanted_all = targets[0]
     wanted_all = lax.all_gather(wanted_all, COL, axis=1, tiled=True)
     first = first_moment[0]

time: 410 us -> 389 us (0.949)
  blocking collectives: 117 us -> 223 us
  waiting for transfers between devices: 202 us -> 103 us
  starting transfers between devices: 35.7 us -> 16.2 us
  local copies, waits for them, and re-layouts: 26.5 us -> 17 us
    all_to_all x3 -> x4, blocking collectives: 18.6 us -> 127 us  [sent_to_all(): return lax.all_to_all(copies, axis, split_axis=0, concat_axis=0, tiled=True)]
    all_gather x1 -> x0, waiting for transfers between devices: 73.2 us -> none  [local(): gathered = lax.all_gather(activations[0], 'row', axis=1, tiled=True)]
    ppermute x0 -> x3, waiting for transfers between devices: none -> 63.4 us  [the longest x2 63.4 us: local(): from_left = lax.ppermute(from_left, 'row', right)]
    all_to_all x4 -> x3, waiting for transfers between devices: 91.7 us -> 39.5 us  [sent_to_all(): return lax.all_to_all(copies, axis, split_axis=0, concat_axis=0, tiled=True)]
    all_gather x1, waiting for transfers between devices: 35.4 us -> 0.02 us  [local(): wanted_all = lax.all_gather(wanted_all, COL, axis=1, tiled=True)]
    all_to_all x4 -> x3, starting transfers between devices: 35.6 us -> 10.7 us  [sent_to_all(): return lax.all_to_all(copies, axis, split_axis=0, concat_axis=0, tiled=True)]
    another operation x4 -> x0, local copies, waits for them, and re-layouts: 6.33 us -> none  [split_up(): return jnp.moveaxis(shard.reshape(*before, count, -1, *after), dim, 0)]
    ppermute x0 -> x3, starting transfers between devices: none -> 5.47 us  [the longest x2 4.11 us: local(): from_left = lax.ppermute(from_left, 'row', right)]
  transfers between devices with their start and end apart: 6 -> 7, of which waited for: 5 -> 5; matrix products, arithmetic and copies ran while one was open for 2% -> 3% of each run, Pallas kernels for 0% -> 0%
where the time goes in v1:
time: 389 us; the launch traced here: 388 us
  blocking collectives  223 us (57%)
  waiting for transfers between devices  103 us (26%)
  local copies, waits for them, and re-layouts  17 us (4%)
  starting transfers between devices  16.2 us (4%)
  between operations  14.5 us (4%)
  matrix products  10.4 us (3%)
  other arithmetic  4.2 us (1%)
    all_to_all x4, blocking collectives, sent_to_all(): return lax.all_to_all(copies, axis, split_axis=0, concat_axis=0, tiled=True)  127 us
    all_to_all x3, blocking collectives, sum_in_two_steps(): return jnp.sum(lax.all_to_all(own, far, 0, 0, tiled=True), axis=0)  76.7 us
    ppermute x2, waiting for transfers between devices, local(): from_left = lax.ppermute(from_left, 'row', right)  63.4 us
    all_to_all x3, waiting for transfers between devices, sent_to_all(): return lax.all_to_all(copies, axis, split_axis=0, concat_axis=0, tiled=True)  39.5 us
    all_to_all x3, blocking collectives, summed_on_arrival(): parts = lax.all_to_all(split_up(shard, dim, count), axis, 0, 0, tiled=True)  19.4 us
    all_to_all x3, starting transfers between devices, sent_to_all(): return lax.all_to_all(copies, axis, split_axis=0, concat_axis=0, tiled=True)  10.7 us
  transfers between devices with their start and end apart: 7, of which 5 were waited for; matrix products, arithmetic and copies ran while one was open for 3% of the time, Pallas kernels for 0%

profile of v1, /device:TPU:1, one launch (start us, length us, event | category | flops | bytes accessed | tf_op | source)
XLA Modules:
  0.0 388.2 jit_solution(4316452791023579407)
XLA Ops:
  7.2 2.1 collective-permute-start
  9.3 1.4 collective-permute-start.1
  10.7 31.9 %collective-permute-done = bf16[3,512,512]{2,1,0:T(8,128)(2,1)S(1)} collective-permute-done((bf16[3,512,512]{2,1,0:T(8,128)(2,1)}, bf16[3,512,512]{2,1,0:T(8,128)(2,1)S(1)}, u32[]{:S(2)}, u32[]{:S(2)}) %collective-permute-start) | collective-permute-done | bytes 1572896 | tf_op jit(solution)/shard_map/ppermute | solution.py:89
  42.6 2.0 collective-permute-start.2
  46.6 31.5 %collective-permute-done.2 = bf16[3,512,512]{2,1,0:T(8,128)(2,1)} collective-permute-done((bf16[3,512,512]{2,1,0:T(8,128)(2,1)S(1)}, bf16[3,512,512]{2,1,0:T(8,128)(2,1)}, u32[]{:S(2)}, u32[]{:S(2)}) %collective-permute-start.2) | collective-permute-done | bytes 1572896 | tf_op jit(solution)/shard_map/ppermute | solution.py:89
  78.0 1.6 constant_dynamic-update-slice_fusion
  79.7 2.5 fusion.43
  82.2 1.4 copy-done
  84.5 8.6 %all_to_all.65 = f32[2,8,128,256]{3,2,1,0:T(8,128)S(1)} all-to-all(f32[2,8,128,256]{3,2,1,0:T(8,128)S(1)} %copy.17), channel_id=1, replica_groups=mesh['grp'=4,'row'=4,'col_0'=4,'col_1'=2,'col_2'=2] {'col_2'}, dimensions={0} | all-to-all | bytes 4194304 | tf_op jit(solution)/shard_map/all_to_all | solution.py:28
  93.4 33.0 %all_to_all.66 = f32[8,128,256]{2,1,0:T(8,128)S(1)} all-to-all(f32[8,128,256]{2,1,0:T(8,128)S(1)} %reduce_sum.63), channel_id=1, replica_groups=mesh['grp'=4,'row'=4,'col_0'=4,'col_1'=2,'col_2'=2] {'col_0','col_1'}, dimensions={0} | all-to-all | bytes 2097152 | tf_op jit(solution)/shard_map/all_to_all | solution.py:35
  127.6 3.6 all-to-all-start.2
  131.2 3.4 fusion.44
  134.5 11.0 %all-to-all-done.2 = f32[8,128,256]{2,1,0:T(8,128)S(1)} async-done(((f32[8,128,256]{2,1,0:T(8,128)}), f32[8,128,256]{2,1,0:T(8,128)S(1)}, u32[]{:S(2)}, u32[]{:S(2)}) %all-to-all-start.2) | async-done | bytes 1048608 | tf_op jit(solution)/shard_map/all_to_all | solution.py:47
  145.7 13.1 %all_to_all.67 = f32[2,8,128,256]{3,2,1,0:T(8,128)S(1)} all-to-all(f32[2,8,128,256]{3,2,1,0:T(8,128)S(1)} %broadcast_in_dim.26), channel_id=1, replica_groups=mesh['grp'=4,'row'=4,'col_0'=4,'col_1'=2,'col_2'=2] {'col_2'}, dimensions={0} | all-to-all | bytes 4194304 | tf_op jit(solution)/shard_map/all_to_all | solution.py:47
  159.2 2.5 fusion.7
  161.8 1.1 convolution_bitcast_fusion.1
  163.1 5.4 %all_to_all.68 = f32[2,8,128,256]{3,2,1,0:T(8,128)S(1)} all-to-all(f32[2,8,128,256]{3,2,1,0:T(8,128)S(1)} %copy.19), channel_id=1, replica_groups=mesh['grp'=4,'row'=4,'col_0'=4,'col_1'=2,'col_2'=2] {'col_2'}, dimensions={0} | all-to-all | bytes 4194304 | tf_op jit(solution)/shard_map/all_to_all | solution.py:28
  168.8 21.9 %all_to_all.69 = f32[8,128,256]{2,1,0:T(8,128)S(1)} all-to-all(f32[8,128,256]{2,1,0:T(8,128)S(1)} %reduce_sum.65), channel_id=1, replica_groups=mesh['grp'=4,'row'=4,'col_0'=4,'col_1'=2,'col_2'=2] {'col_0','col_1'}, dimensions={0} | all-to-all | bytes 2097152 | tf_op jit(solution)/shard_map/all_to_all | solution.py:35
  190.7 1.1 broadcast_in_dim.27
  191.8 3.6 all-to-all-start.6
  195.4 14.3 %all-to-all-done.6 = f32[8,128,256]{2,1,0:T(8,128)S(1)} async-done(((f32[8,128,256]{2,1,0:T(8,128)}), f32[8,128,256]{2,1,0:T(8,128)S(1)}, u32[]{:S(2)}, u32[]{:S(2)}) %all-to-all-start.6) | async-done | bytes 1048608 | tf_op jit(solution)/shard_map/all_to_all | solution.py:47
  209.9 15.1 %all_to_all.70 = f32[2,8,128,256]{3,2,1,0:T(8,128)S(1)} all-to-all(f32[2,8,128,256]{3,2,1,0:T(8,128)S(1)} %broadcast_in_dim.28), channel_id=1, replica_groups=mesh['grp'=4,'row'=4,'col_0'=4,'col_1'=2,'col_2'=2] {'col_2'}, dimensions={0} | all-to-all | bytes 4194304 | tf_op jit(solution)/shard_map/all_to_all | solution.py:47
  225.4 2.5 fusion.5
  228.1 1.5 convolution_bitcast_fusion
  229.8 5.4 %all_to_all.71 = f32[2,8,128,256]{3,2,1,0:T(8,128)S(1)} all-to-all(f32[2,8,128,256]{3,2,1,0:T(8,128)S(1)} %copy.21), channel_id=1, replica_groups=mesh['grp'=4,'row'=4,'col_0'=4,'col_1'=2,'col_2'=2] {'col_2'}, dimensions={0} | all-to-all | bytes 4194304 | tf_op jit(solution)/shard_map/all_to_all | solution.py:28
  235.4 21.8 %all_to_all.72 = f32[8,128,256]{2,1,0:T(8,128)S(1)} all-to-all(f32[8,128,256]{2,1,0:T(8,128)S(1)} %reduce_sum.67), channel_id=1, replica_groups=mesh['grp'=4,'row'=4,'col_0'=4,'col_1'=2,'col_2'=2] {'col_0','col_1'}, dimensions={0} | all-to-all | bytes 2097152 | tf_op jit(solution)/shard_map/all_to_all | solution.py:35
  258.3 3.6 all-to-all-start.10
  261.9 14.2 %all-to-all-done.10 = f32[8,128,256]{2,1,0:T(8,128)S(1)} async-done(((f32[8,128,256]{2,1,0:T(8,128)}), f32[8,128,256]{2,1,0:T(8,128)S(1)}, u32[]{:S(2)}, u32[]{:S(2)}) %all-to-all-start.10) | async-done | bytes 1048608 | tf_op jit(solution)/shard_map/all_to_all | solution.py:47
  276.4 16.3 %all_to_all.73 = f32[2,8,128,256]{3,2,1,0:T(8,128)S(1)} all-to-all(f32[2,8,128,256]{3,2,1,0:T(8,128)S(1)} %broadcast_in_dim.30), channel_id=1, replica_groups=mesh['grp'=4,'row'=4,'col_0'=4,'col_1'=2,'col_2'=2] {'col_2'}, dimensions={0} | all-to-all | bytes 4194304 | tf_op jit(solution)/shard_map/all_to_all | solution.py:47
  294.4 2.1 fusion.10
  296.6 82.4 %all_to_all.74 = f32[4,512,256]{2,1,0:T(8,128)S(1)} all-to-all(f32[4,512,256]{2,1,0:T(8,128)S(1)} %broadcast_in_dim.31), channel_id=1, replica_groups=mesh['grp'=4,'row'=4,'col_0'=4,'col_1'=2,'col_2'=2] {'grp'}, dimensions={0} | all-to-all | bytes 4194304 | tf_op jit(solution)/shard_map/all_to_all | solution.py:47
  379.2 2.1 multiply_subtract_fusion
  (74 shorter events, 9.9 us)
Async XLA Ops:
  7.2 124.0 %all-gather.3.cloned.1.call-start = ((), (), s32[]{:S(2)}) async-start(), calls=%async_computation.13 | async-start | bytes 3342336 | tf_op jit(solution)/shard_map/all_gather | solution.py:98
  7.2 35.4 %collective-permute-start = (bf16[3,512,512]{2,1,0:T(8,128)(2,1)}, bf16[3,512,512]{2,1,0:T(8,128)(2,1)S(1)}, u32[]{:S(2)}, u32[]{:S(2)}) collective-permute-start(bf16[3,512,512]{2,1,0:T(8,128)(2,1)} %bitcast.93), channel_id=1, source_target_pairs={{0,16},{16,32},{32,48},{48,0},{1,17},{17,33},{33,49},{49,1},{2,18}... | collective-permute-start | bytes 4718600 | tf_op jit(solution)/shard_map/ppermute | solution.py:89
  9.3 37.1 %collective-permute-start.1 = (bf16[3,512,512]{2,1,0:T(8,128)(2,1)}, bf16[3,512,512]{2,1,0:T(8,128)(2,1)S(1)}, u32[]{:S(2)}, u32[]{:S(2)}) collective-permute-start(bf16[3,512,512]{2,1,0:T(8,128)(2,1)} %bitcast.94), channel_id=1, source_target_pairs={{0,48},{16,0},{32,16},{48,32},{1,49},{17,1},{33,17},{49,33},{2,50}... | collective-permute-start | bytes 4718600 | tf_op jit(solution)/shard_map/ppermute | solution.py:92
  42.6 35.4 %collective-permute-start.2 = (bf16[3,512,512]{2,1,0:T(8,128)(2,1)S(1)}, bf16[3,512,512]{2,1,0:T(8,128)(2,1)}, u32[]{:S(2)}, u32[]{:S(2)}) collective-permute-start(bf16[3,512,512]{2,1,0:T(8,128)(2,1)S(1)} %collective-permute-done), channel_id=1, source_target_pairs={{0,16},{16,32},{32,48},{48,0},{1,17},{17,33},{33,49},{49,1},{2,18}... | collective-permute-start | bytes 4718600 | tf_op jit(solution)/shard_map/ppermute | solution.py:89
  44.6 1.4 copy-start.9
  79.7 3.9 %copy-start = (bf16[3,2048,512]{2,1,0:T(8,128)(2,1)}, bf16[3,2048,512]{2,1,0:T(8,128)(2,1)S(1)}, u32[]{:S(2)}) copy-start(bf16[3,2048,512]{2,1,0:T(8,128)(2,1)S(1)} %constant_dynamic-update-slice_fusion) | copy-start | bytes 18874372
  79.7 3.9 %copy-start.3 = (f32[512,256]{1,0:T(8,128)S(1)}, f32[512,256]{1,0:T(8,128)}, u32[]{:S(2)}) copy-start(f32[512,256]{1,0:T(8,128)} %param.6) | copy-start | bytes 1572868
  127.6 18.0 %all-to-all-start.2 = ((f32[8,128,256]{2,1,0:T(8,128)}), f32[8,128,256]{2,1,0:T(8,128)S(1)}, u32[]{:S(2)}, u32[]{:S(2)}) async-start(f32[8,128,256]{2,1,0:T(8,128)} %broadcast_in_dim.25), calls=%async_computation.2 | async-start | bytes 2097152 | tf_op jit(solution)/shard_map/all_to_all | solution.py:47
  159.2 2.6 copy-start.4
  159.2 2.5 copy-start.8
  159.2 2.5 copy-start.10
  159.2 2.6 copy-start.13
  161.7 1.2 copy-start.16
  191.8 17.9 %all-to-all-start.6 = ((f32[8,128,256]{2,1,0:T(8,128)}), f32[8,128,256]{2,1,0:T(8,128)S(1)}, u32[]{:S(2)}, u32[]{:S(2)}) async-start(f32[8,128,256]{2,1,0:T(8,128)} %broadcast_in_dim.27), calls=%async_computation.6 | async-start | bytes 2097152 | tf_op jit(solution)/shard_map/all_to_all | solution.py:47
  209.9 15.1 %copy-start.2 = (bf16[1,1,2048,256]{3,2,1,0:T(8,128)(2,1)S(1)}, bf16[1,1,2048,256]{3,2,1,0:T(8,128)(2,1)}, u32[]{:S(2)}) copy-start(bf16[1,1,2048,256]{3,2,1,0:T(8,128)(2,1)} %get-tuple-element.8) | copy-start | bytes 3145732
  225.3 2.6 copy-start.5
  225.3 2.6 copy-start.7
  225.3 2.6 copy-start.11
  225.4 2.6 copy-start.14
  225.4 2.7 copy-start.17
  227.9 1.8 copy-start.19
  258.3 17.8 %all-to-all-start.10 = ((f32[8,128,256]{2,1,0:T(8,128)}), f32[8,128,256]{2,1,0:T(8,128)S(1)}, u32[]{:S(2)}, u32[]{:S(2)}) async-start(f32[8,128,256]{2,1,0:T(8,128)} %broadcast_in_dim.29), calls=%async_computation.10 | async-start | bytes 2097152 | tf_op jit(solution)/shard_map/all_to_all | solution.py:47
  276.1 16.9 %slice-start = ((s8[6291456]{0:T(1024)(128)(4,1)}), s8[4194304]{0:T(1024)(128)(4,1)S(1)}, s32[]{:S(2)}) async-start(s8[6291456]{0:T(1024)(128)(4,1)} %bitcast.85), calls=%async_computation.14 | async-start | bytes 8388608
  276.4 16.3 %copy-start.1 = (bf16[1,1,2048,256]{3,2,1,0:T(8,128)(2,1)S(1)}, bf16[1,1,2048,256]{3,2,1,0:T(8,128)(2,1)}, u32[]{:S(2)}) copy-start(bf16[1,1,2048,256]{3,2,1,0:T(8,128)(2,1)} %get-tuple-element.9) | copy-start | bytes 3145732
  276.4 16.7 %slice-start.1 = ((s8[6291456]{0:T(1024)(128)(4,1)}), s8[2097152]{0:T(1024)(128)(4,1)S(1)}, s32[]{:S(2)}) async-start(s8[6291456]{0:T(1024)(128)(4,1)} %bitcast.85), calls=%async_computation.15 | async-start | bytes 4194304
  292.7 1.0 copy-start.6
  292.7 1.2 copy-start.12
  292.7 1.4 copy-start.15
  292.7 1.5 copy-start.18
  292.7 1.7 copy-start.20
Sparse Core Ops, SparseCore 0:
  10.8 74.4 all-gather.2
